TPU v7x, 32 devices: a whole 2x2x4 slice. The times are simulated.
32 devices in a mesh: mom: 4 (over y, x), sec: 8 (over z, core).
Axes of the slice: x: 2, y: 2, z: 4, core: 2. Of those that a mesh axis runs over, the one named last changes fastest.
Arguments:
- left_env: bfloat16 [64, 64, 2816], P('sec', 'mom'), may hold values from -0.75 to 0.75
- right_env: bfloat16 [64, 64, 2816], P('sec', 'mom'), may hold values from -0.109375 to 0.109375
- left_mixed: bfloat16 [4, 64, 64, 2816], P('mom', 'sec'), may hold values from -0.75 to 0.75
- excitation: bfloat16 [4, 64, 64, 256], P('mom', 'sec'), may hold values from -6 to 6
- ground: bfloat16 [64, 64, 256], P('sec'), may hold values from -6 to 6
- mpo: bfloat16 [44, 4, 44, 4], replicated, may hold values from -0.4375 to 0.4375
- momentum: int32 [4], P('mom'), may hold values from 0 to 3, each once
- block_dims: int32 [64], P('sec'), may hold values from 16 to 64, as said below
Outputs:
- excited: bfloat16 [4, 2, 64, 64, 256], P('mom', None, 'sec')
Inputs may be any that keep to these rules, and one draw needn't show every extreme that they name: `block_dims`: every block has at least 16 used rows; some block uses all 64 and some exactly 16.
All inputs are finite; a program needn't handle non-finite values.
Results may differ from a plain program's by a relative error of at most 0.0058.
Values may be sent and summed in bfloat16 or wider, within the bound.
No kernel may reach another device: no remote copies, remote signals or barrier semaphores. Data moves between devices by JAX's collectives and lax.ppermute only.
A program may use at most 128 MiB of HBM per device.

v0:
```python
import math
import jax
import jax.numpy as jnp
from jax import lax
from jax.sharding import PartitionSpec as P


def with_halo(shard, sides, width):
    for axis, dim in sides:
        devices, length = (lax.axis_size(axis), shard.shape[dim])
        up = [(i, (i + 1) % devices) for i in range(devices - 1)]
        down = [(j, i) for i, j in up]
        last = lax.slice_in_dim(shard, length - width, length, axis=dim)
        initial = lax.slice_in_dim(shard, 0, width, axis=dim)
        before = lax.ppermute(last, axis, up)
        after = lax.ppermute(initial, axis, down)
        shard = jnp.concatenate([before, shard, after], axis=dim)
    return shard


def apply_term(left, source, right, mpo):
    width = left.shape[1]
    low = width // 3
    high = width - low
    bounds = [(0, low), (low, high), (high, width)]
    count = source.shape[0]
    rows = left.shape[0]
    block = right.shape[0]
    wide = source.shape[-1]
    phys = wide // block
    total = None
    for shift in range(3):
        start, stop = bounds[shift]
        temp = jnp.einsum(
            "iwa,nab->niwb",
            left[:, start:stop, :],
            source[:, shift],
            preferred_element_type=jnp.float32,
        ).astype(jnp.bfloat16)
        temp = temp.reshape(count, rows, stop - start, phys, block)
        part_sum = jnp.einsum(
            "niwpj,wpvq->nviqj", temp, mpo[start:stop], preferred_element_type=jnp.float32
        )
        total = part_sum if total is None else total + part_sum
    mixed = total.astype(jnp.bfloat16)
    result = jnp.einsum("nviqj,jvk->niqk", mixed, right, preferred_element_type=jnp.float32)
    return result.reshape(count, rows, wide)


def shards(left_env, right_env, left_mixed, excitation, ground, mpo, momentum, block_dims):
    sectors = excitation.shape[1]
    block = excitation.shape[2]
    wide = excitation.shape[3]
    width = left_env.shape[2] // block
    groups = lax.axis_size("mom")
    right_full = lax.all_gather(right_env, "mom", axis=1, tiled=True)
    stacked = jnp.stack([excitation[0], ground])
    padded = with_halo(stacked, (("sec", 1),), 1)
    sector_ids = jnp.arange(sectors, dtype=jnp.int32)

    def shifted_sector(sector):
        right = right_full[sector].reshape(block, width, block)
        mixl = left_mixed[0, sector].reshape(block, width, block)
        src = lax.dynamic_slice_in_dim(padded[1:2], sector, 3, 1)
        return apply_term(mixl, src, right, mpo)[0]

    shifted = lax.map(shifted_sector, sector_ids)
    left_full = lax.all_gather(left_env, "mom", axis=1, tiled=True)

    def direct_sector(sector):
        right = right_full[sector].reshape(block, width, block)
        left = left_full[sector].reshape(block, width, block)
        src = lax.dynamic_slice_in_dim(padded[0:1], sector, 3, 1)
        return apply_term(left, src, right, mpo)[0]

    direct = lax.map(direct_sector, sector_ids)
    phase = 2.0 * math.pi * momentum[0].astype(jnp.float32) / groups
    rows_idx = jnp.arange(block, dtype=jnp.int32)
    cols_idx = jnp.arange(wide, dtype=jnp.int32) % block
    used = block_dims[:, None, None]
    mask = ((rows_idx[None, :, None] < used) & (cols_idx[None, None, :] < used)).astype(jnp.float32)
    real_part = mask * (direct + jnp.cos(phase) * shifted)
    imag_part = -mask * jnp.sin(phase) * shifted
    return jnp.stack([real_part, imag_part])[None].astype(jnp.bfloat16)


def solution(mesh):
    return jax.shard_map(
        shards,
        mesh=mesh,
        in_specs=(
            P("sec", "mom", None),
            P("sec", "mom", None),
            P("mom", "sec", None, None),
            P("mom", "sec", None, None),
            P("sec", None, None),
            P(),
            P("mom"),
            P("sec"),
        ),
        out_specs=P("mom", None, "sec", None, None),
        check_vma=False,
    )
```

profile of v0, /device:TPU:0, one launch (start us, length us, event | category | flops | bytes accessed | tf_op | source)
XLA Modules:
  0.0 640.0 jit_solution(17581412542030367887)
XLA Ops:
  18.7 35.0 %all-gather.3.cloned.1.call-done = bf16[8,64,2816]{2,1,0:T(8,128)(2,1)} async-done(((bf16[8,16,2816]{2,1,0:T(8,128)(2,1)}), bf16[8,64,2816]{2,1,0:T(8,128)(2,1)}) %all-gather.3.cloned.1.call-update) | async-done | bytes 2883600 | tf_op jit(solution)/shard_map/all_gather | solution.py:68
  53.7 43.7 %all-gather.5.cloned.1.call-done = bf16[8,64,2816]{2,1,0:T(8,128)(2,1)} async-done(((bf16[8,16,2816]{2,1,0:T(8,128)(2,1)}), bf16[8,64,2816]{2,1,0:T(8,128)(2,1)}) %all-gather.5.cloned.1.call-update) | async-done | bytes 2883600 | tf_op jit(solution)/shard_map/all_gather | solution.py:56
  98.3 268.4 %while.20 = (s32[]{:T(128)}, f32[8,64,256]{2,1,0:T(8,128)}, bf16[2,10,64,256]{3,2,1,0:T(8,128)(2,1)S(1)}, s32[8]{0:T(128)S(1)}, bf16[8,64,2816]{2,1,0:T(8,128)(2...) while((s32[]{:T(128)}, f32[8,64,256]{2,1,0:T(8,128)}, ...), condition=%wide.region_1.2_spmd, body=%wide.region_0.1_spmd.sunk | while | flops 441188352 | bytes 44241284 | solution.py:76
  104.7 3.7 fusion.105
  115.9 6.3 fusion.110
  122.3 5.2 copy.125
  138.2 3.7 fusion.105
  143.5 3.7 fusion.108
  149.5 6.3 fusion.110
  155.8 5.2 copy.125
  171.8 3.7 fusion.105
  177.0 3.7 fusion.108
  183.0 6.3 fusion.110
  189.4 5.2 copy.125
  205.3 3.7 fusion.105
  210.6 3.7 fusion.108
  216.6 6.3 fusion.110
  222.9 5.2 copy.125
  238.9 3.7 fusion.105
  244.1 3.7 fusion.108
  250.1 6.3 fusion.110
  256.5 5.2 copy.125
  272.5 3.7 fusion.105
  277.7 3.7 fusion.108
  283.7 6.3 fusion.110
  290.0 5.2 copy.125
  306.0 3.7 fusion.105
  311.2 3.7 fusion.108
  317.3 6.3 fusion.110
  323.6 5.2 copy.125
  339.6 3.7 fusion.105
  344.8 3.7 fusion.108
  350.8 6.3 fusion.110
  357.2 5.2 copy.125
  367.5 263.4 %while.21 = (s32[]{:T(128)}, f32[8,64,256]{2,1,0:T(8,128)}, bf16[2,10,64,256]{3,2,1,0:T(8,128)(2,1)S(1)}, s32[8]{0:T(128)S(1)}, bf16[1,8,64,2816]{3,2,1,0:T(8,12...) while((s32[]{:T(128)}, f32[8,64,256]{2,1,0:T(8,128)}, ...), condition=%wide.region_3.4_spmd, body=%wide.region_2.3_spmd.sunk | while | flops 441188352 | bytes 43225452 | solution.py:67
  373.8 3.7 fusion.123
  378.2 3.7 fusion.126
  383.5 6.3 fusion.128
  389.8 5.2 copy.133
  406.7 3.7 fusion.123
  411.2 3.7 fusion.126
  416.4 6.3 fusion.128
  422.8 5.2 copy.133
  439.6 3.7 fusion.123
  444.1 3.7 fusion.126
  449.3 6.3 fusion.128
  455.7 5.2 copy.133
  472.5 3.7 fusion.123
  482.3 6.3 fusion.128
  488.6 5.2 copy.133
  505.5 3.7 fusion.123
  515.2 6.3 fusion.128
  521.5 5.2 copy.133
  538.4 3.7 fusion.123
  542.9 3.7 fusion.126
  548.1 6.3 fusion.128
  554.5 5.2 copy.133
  571.3 3.7 fusion.123
  581.1 6.3 fusion.128
  587.4 5.2 copy.133
  604.3 3.7 fusion.123
  608.8 3.7 fusion.126
  614.0 6.3 fusion.128
  620.3 5.2 copy.133
  (452 shorter events, 205.8 us)
Async XLA Ops:
  6.5 47.2 %all-gather.3.cloned.1.call-start = ((), (), s32[]{:S(2)}) async-start(), calls=%async_computation | async-start | bytes 3604480 | tf_op jit(solution)/shard_map/all_gather | solution.py:68
  7.3 90.2 %all-gather.5.cloned.1.call-start = ((), (), s32[]{:S(2)}) async-start(), calls=%async_computation.1 | async-start | bytes 3604480 | tf_op jit(solution)/shard_map/all_gather | solution.py:56
  8.8 8.7 %collective-permute-start.1 = (bf16[2,1,64,256]{3,2,1,0:T(8,128)(2,1)S(1)}, bf16[2,1,64,256]{3,2,1,0:T(8,128)(2,1)S(1)}, u32[]{:S(2)}, u32[]{:S(2)}) collective-permute-start(bf16[2,1,64,256]{3,2,1,0:T(8,128)(2,1)S(1)} %get-tuple-element.146), channel_id=1, source_target_pairs={{1,0},{2,1},{3,2},{4,3},{5,4},{6,5},{7,6},{9,8},{10,9},{11,10},{12... | collective-permute-start | bytes 196616 | tf_op jit(solution)/shard_map/ppermute | solution.py:16
  10.1 7.4 %collective-permute-start = (bf16[2,1,64,256]{3,2,1,0:T(8,128)(2,1)S(1)}, bf16[2,1,64,256]{3,2,1,0:T(8,128)(2,1)S(1)}, u32[]{:S(2)}, u32[]{:S(2)}) collective-permute-start(bf16[2,1,64,256]{3,2,1,0:T(8,128)(2,1)S(1)} %get-tuple-element.145), channel_id=1, source_target_pairs={{0,1},{1,2},{2,3},{3,4},{4,5},{5,6},{6,7},{8,9},{9,10},{10,11},{11... | collective-permute-start | bytes 196616 | tf_op jit(solution)/shard_map/ppermute | solution.py:15
  98.3 5.7 copy-start.4
  98.3 11.6 %copy-start = (bf16[44,4,44,4]{2,0,1,3:T(8,128)(2,1)}, bf16[44,4,44,4]{2,0,1,3:T(8,128)(2,1)S(1)}, u32[]{:S(2)}) copy-start(bf16[44,4,44,4]{2,0,1,3:T(8,128)(2,1)S(1)} %get-tuple-element.276) | copy-start | bytes 185860 | tf_op jit(solution)/shard_map/while
  127.5 4.3 copy-start.1
  127.5 4.3 copy-start.5
  131.8 5.7 copy-start.4
  131.8 11.6 %copy-start = (bf16[44,4,44,4]{2,0,1,3:T(8,128)(2,1)}, bf16[44,4,44,4]{2,0,1,3:T(8,128)(2,1)S(1)}, u32[]{:S(2)}) copy-start(bf16[44,4,44,4]{2,0,1,3:T(8,128)(2,1)S(1)} %get-tuple-element.276) | copy-start | bytes 185860 | tf_op jit(solution)/shard_map/while
  161.0 4.3 copy-start.1
  161.0 4.3 copy-start.5
  165.4 5.7 copy-start.4
  165.4 11.6 %copy-start = (bf16[44,4,44,4]{2,0,1,3:T(8,128)(2,1)}, bf16[44,4,44,4]{2,0,1,3:T(8,128)(2,1)S(1)}, u32[]{:S(2)}) copy-start(bf16[44,4,44,4]{2,0,1,3:T(8,128)(2,1)S(1)} %get-tuple-element.276) | copy-start | bytes 185860 | tf_op jit(solution)/shard_map/while
  194.6 4.3 copy-start.1
  194.6 4.3 copy-start.5
  198.9 5.7 copy-start.4
  198.9 11.6 %copy-start = (bf16[44,4,44,4]{2,0,1,3:T(8,128)(2,1)}, bf16[44,4,44,4]{2,0,1,3:T(8,128)(2,1)S(1)}, u32[]{:S(2)}) copy-start(bf16[44,4,44,4]{2,0,1,3:T(8,128)(2,1)S(1)} %get-tuple-element.276) | copy-start | bytes 185860 | tf_op jit(solution)/shard_map/while
  228.2 4.3 copy-start.1
  228.2 4.3 copy-start.5
  232.5 5.7 copy-start.4
  232.5 11.6 %copy-start = (bf16[44,4,44,4]{2,0,1,3:T(8,128)(2,1)}, bf16[44,4,44,4]{2,0,1,3:T(8,128)(2,1)S(1)}, u32[]{:S(2)}) copy-start(bf16[44,4,44,4]{2,0,1,3:T(8,128)(2,1)S(1)} %get-tuple-element.276) | copy-start | bytes 185860 | tf_op jit(solution)/shard_map/while
  261.7 4.3 copy-start.1
  261.7 4.3 copy-start.5
  266.0 5.7 copy-start.4
  266.0 11.6 %copy-start = (bf16[44,4,44,4]{2,0,1,3:T(8,128)(2,1)}, bf16[44,4,44,4]{2,0,1,3:T(8,128)(2,1)S(1)}, u32[]{:S(2)}) copy-start(bf16[44,4,44,4]{2,0,1,3:T(8,128)(2,1)S(1)} %get-tuple-element.276) | copy-start | bytes 185860 | tf_op jit(solution)/shard_map/while
  295.3 4.3 copy-start.5
  299.6 5.7 copy-start.4
  299.6 11.6 %copy-start = (bf16[44,4,44,4]{2,0,1,3:T(8,128)(2,1)}, bf16[44,4,44,4]{2,0,1,3:T(8,128)(2,1)S(1)}, u32[]{:S(2)}) copy-start(bf16[44,4,44,4]{2,0,1,3:T(8,128)(2,1)S(1)} %get-tuple-element.276) | copy-start | bytes 185860 | tf_op jit(solution)/shard_map/while
  328.8 4.3 copy-start.5
  333.1 5.7 copy-start.4
  333.2 11.6 %copy-start = (bf16[44,4,44,4]{2,0,1,3:T(8,128)(2,1)}, bf16[44,4,44,4]{2,0,1,3:T(8,128)(2,1)S(1)}, u32[]{:S(2)}) copy-start(bf16[44,4,44,4]{2,0,1,3:T(8,128)(2,1)S(1)} %get-tuple-element.276) | copy-start | bytes 185860 | tf_op jit(solution)/shard_map/while
  362.4 4.3 copy-start.1
  362.4 4.3 copy-start.5
  367.5 263.4 %copy-start.9 = (pred[8,256]{1,0:T(8,128)(4,1)S(1)}, pred[8,256]{1,0:T(8,128)(4,1)}, u32[]{:S(2)}) copy-start(pred[8,256]{1,0:T(8,128)(4,1)} %broadcast_compare_fusion) | copy-start | bytes 6148
  367.5 263.4 %copy-start.10 = (pred[8,64]{1,0:T(8,128)(4,1)S(1)}, pred[8,64]{1,0:T(8,128)(4,1)}, u32[]{:S(2)}) copy-start(pred[8,64]{1,0:T(8,128)(4,1)} %iota_compare_fusion) | copy-start | bytes 1540
  367.5 5.5 copy-start.6
  367.5 10.7 %copy-start.2 = (bf16[44,4,44,4]{2,0,1,3:T(8,128)(2,1)}, bf16[44,4,44,4]{2,0,1,3:T(8,128)(2,1)S(1)}, u32[]{:S(2)}) copy-start(bf16[44,4,44,4]{2,0,1,3:T(8,128)(2,1)S(1)} %get-tuple-element.315) | copy-start | bytes 185860 | tf_op jit(solution)/shard_map/while
  396.1 4.3 copy-start.3
  400.4 5.6 copy-start.6
  400.4 10.8 %copy-start.2 = (bf16[44,4,44,4]{2,0,1,3:T(8,128)(2,1)}, bf16[44,4,44,4]{2,0,1,3:T(8,128)(2,1)S(1)}, u32[]{:S(2)}) copy-start(bf16[44,4,44,4]{2,0,1,3:T(8,128)(2,1)S(1)} %get-tuple-element.315) | copy-start | bytes 185860 | tf_op jit(solution)/shard_map/while
  429.0 4.3 copy-start.3
  433.3 5.6 copy-start.6
  433.3 10.8 %copy-start.2 = (bf16[44,4,44,4]{2,0,1,3:T(8,128)(2,1)}, bf16[44,4,44,4]{2,0,1,3:T(8,128)(2,1)S(1)}, u32[]{:S(2)}) copy-start(bf16[44,4,44,4]{2,0,1,3:T(8,128)(2,1)S(1)} %get-tuple-element.315) | copy-start | bytes 185860 | tf_op jit(solution)/shard_map/while
  461.9 4.3 copy-start.3
  466.2 5.6 copy-start.6
  466.2 10.8 %copy-start.2 = (bf16[44,4,44,4]{2,0,1,3:T(8,128)(2,1)}, bf16[44,4,44,4]{2,0,1,3:T(8,128)(2,1)S(1)}, u32[]{:S(2)}) copy-start(bf16[44,4,44,4]{2,0,1,3:T(8,128)(2,1)S(1)} %get-tuple-element.315) | copy-start | bytes 185860 | tf_op jit(solution)/shard_map/while
  494.8 4.3 copy-start.3
  499.2 5.6 copy-start.6
  499.2 10.8 %copy-start.2 = (bf16[44,4,44,4]{2,0,1,3:T(8,128)(2,1)}, bf16[44,4,44,4]{2,0,1,3:T(8,128)(2,1)S(1)}, u32[]{:S(2)}) copy-start(bf16[44,4,44,4]{2,0,1,3:T(8,128)(2,1)S(1)} %get-tuple-element.315) | copy-start | bytes 185860 | tf_op jit(solution)/shard_map/while
  527.8 4.3 copy-start.3
  527.8 4.3 copy-start.7
  532.1 5.6 copy-start.6
  532.1 10.8 %copy-start.2 = (bf16[44,4,44,4]{2,0,1,3:T(8,128)(2,1)}, bf16[44,4,44,4]{2,0,1,3:T(8,128)(2,1)S(1)}, u32[]{:S(2)}) copy-start(bf16[44,4,44,4]{2,0,1,3:T(8,128)(2,1)S(1)} %get-tuple-element.315) | copy-start | bytes 185860 | tf_op jit(solution)/shard_map/while
  560.7 4.3 copy-start.3
  560.7 4.3 copy-start.7
  565.0 5.6 copy-start.6
  565.0 10.8 %copy-start.2 = (bf16[44,4,44,4]{2,0,1,3:T(8,128)(2,1)}, bf16[44,4,44,4]{2,0,1,3:T(8,128)(2,1)S(1)}, u32[]{:S(2)}) copy-start(bf16[44,4,44,4]{2,0,1,3:T(8,128)(2,1)S(1)} %get-tuple-element.315) | copy-start | bytes 185860 | tf_op jit(solution)/shard_map/while
  593.7 4.3 copy-start.3
  593.7 4.3 copy-start.7
  598.0 5.6 copy-start.6
  598.0 10.8 %copy-start.2 = (bf16[44,4,44,4]{2,0,1,3:T(8,128)(2,1)}, bf16[44,4,44,4]{2,0,1,3:T(8,128)(2,1)S(1)}, u32[]{:S(2)}) copy-start(bf16[44,4,44,4]{2,0,1,3:T(8,128)(2,1)S(1)} %get-tuple-element.315) | copy-start | bytes 185860 | tf_op jit(solution)/shard_map/while
  626.6 4.3 copy-start.3
  626.6 4.3 copy-start.7
  (14 other events, 41.6 us)
Sparse Core Ops, SparseCore 0:
  9.2 44.4 all-gather.2
  55.6 41.7 all-gather.4
where the time goes:
time: 643 us; the launch traced here: 640 us
  matrix products  291 us (45%)
  local copies, waits for them, and re-layouts  191 us (30%)
  waiting for transfers between devices  80.1 us (12%)
  loops' own time  52.6 us (8%)
  between operations  14.3 us (2%)
  other arithmetic  6.82 us (1%)
    dot_general x48, matrix products, apply_term(): jnp.einsum('niwpj,wpvq->nviqj', temp, mpo[start:stop], preferred_element_...  220 us
    another operation x66, local copies, waits for them, and re-layouts  119 us
    dot_general x16, matrix products, apply_term(): jnp.einsum('nviqj,jvk->niqk', mixed, right, preferred_element_type=jnp.fl...  46.1 us
    all_gather x1, waiting for transfers between devices, shards(): right_full = lax.all_gather(right_env, 'mom', axis=1, tiled=True)  43.7 us
    all_gather x1, waiting for transfers between devices, shards(): left_full = lax.all_gather(left_env, 'mom', axis=1, tiled=True)  35 us
    another operation x1, loops' own time, shards(): shifted = lax.map(shifted_sector, sector_ids)  26.6 us
    another operation x1, loops' own time, shards(): direct = lax.map(direct_sector, sector_ids)  26 us
    dot_general x48, matrix products, apply_term(): jnp.einsum('iwa,nab->niwb', left[:, start:stop, :], source[:, shift], pre...  25 us
  transfers between devices with their start and end apart: 4, of which 2 were waited for; matrix products, arithmetic and copies ran while one was open for 1% of the time, Pallas kernels for 0%

commit v1 on v0

--- a/solution.py
+++ b/solution.py
@@ -53,7 +53,19 @@
     wide = excitation.shape[3]
     width = left_env.shape[2] // block
     groups = lax.axis_size("mom")
-    right_full = lax.all_gather(right_env, "mom", axis=1, tiled=True)
+    arr_now = lax.axis_size("mom")
+    ready = lax.axis_index("mom")
+    out_arr, near = (arr_now, ready)
+    right_full, answer = (right_env, 1)
+    while answer < out_arr:
+        windows = []
+        for ii in range(out_arr):
+            windows.append((ii, ii ^ answer))
+        formed = lax.ppermute(right_full, "mom", perm=windows)
+        block_next = jnp.concatenate([right_full, formed], axis=1)
+        state_now = jnp.concatenate([formed, right_full], axis=1)
+        right_full = jnp.where(near & answer == 0, block_next, state_now)
+        answer = 2 * answer
     stacked = jnp.stack([excitation[0], ground])
     padded = with_halo(stacked, (("sec", 1),), 1)
     sector_ids = jnp.arange(sectors, dtype=jnp.int32)

time: 643 us -> 621 us (0.966)
  waiting for transfers between devices: 80.1 us -> 47.7 us
    ppermute x0 -> x2, waiting for transfers between devices: none -> 47.7 us  [shards(): formed = lax.ppermute(right_full, 'mom', perm=windows)]
    all_gather x1 -> x0, waiting for transfers between devices: 43.7 us -> none  [shards(): right_full = lax.all_gather(right_env, 'mom', axis=1, tiled=True)]
    all_gather x1, waiting for transfers between devices: 35 us -> 0.01 us  [shards(): left_full = lax.all_gather(left_env, 'mom', axis=1, tiled=True)]
    dot_general x48, matrix products: 220 us -> 233 us  [apply_term(): jnp.einsum('niwpj,wpvq->nviqj', temp, mpo[start:stop], preferred_element_...]
    dot_general x48, matrix products: 25 us -> 12.9 us  [apply_term(): jnp.einsum('iwa,nab->niwb', left[:, start:stop, :], source[:, shift], pre...]
  transfers between devices with their start and end apart: 4 -> 5, of which waited for: 2 -> 2; matrix products, arithmetic and copies ran while one was open for 1% -> 39% of each run, Pallas kernels for 0% -> 0%
where the time goes in v1:
time: 621 us; the launch traced here: 618 us
  matrix products  293 us (47%)
  local copies, waits for them, and re-layouts  191 us (31%)
  loops' own time  54.3 us (9%)
  waiting for transfers between devices  47.7 us (8%)
  between operations  14.3 us (2%)
  other arithmetic  9.74 us (2%)
  starting transfers between devices  9.2 us (1%)
    dot_general x48, matrix products, apply_term(): jnp.einsum('niwpj,wpvq->nviqj', temp, mpo[start:stop], preferred_element_...  233 us
    another operation x66, local copies, waits for them, and re-layouts  119 us
    ppermute x2, waiting for transfers between devices, shards(): formed = lax.ppermute(right_full, 'mom', perm=windows)  47.7 us
    dot_general x16, matrix products, apply_term(): jnp.einsum('nviqj,jvk->niqk', mixed, right, preferred_element_type=jnp.fl...  46.4 us
    another operation x1, loops' own time, shards(): shifted = lax.map(shifted_sector, sector_ids)  27.9 us
    another operation x1, loops' own time, shards(): direct = lax.map(direct_sector, sector_ids)  26.5 us
    dot_general x48, matrix products, apply_term(): jnp.einsum('iwa,nab->niwb', left[:, start:stop, :], source[:, shift], pre...  12.9 us
  transfers between devices with their start and end apart: 5, of which 2 were waited for; matrix products, arithmetic and copies ran while one was open for 39% of the time, Pallas kernels for 0%

profile of v1, /device:TPU:0, one launch (start us, length us, event | category | flops | bytes accessed | tf_op | source)
XLA Modules:
  0.0 618.5 jit_solution(10491832465465088563)
XLA Ops:
  9.6 16.3 %collective-permute-done.2 = bf16[8,16,2816]{2,1,0:T(8,128)(2,1)S(1)} collective-permute-done((bf16[8,16,2816]{2,1,0:T(8,128)(2,1)}, bf16[8,16,2816]{2,1,0:T(8,128)(2,1)S(1)}, u32[]{:S(2)}, u32[]{:S(2)}) %collective-permute-start.2) | collective-permute-done | bytes 720928 | tf_op jit(solution)/shard_map/ppermute | solution.py:64
  36.9 31.3 %collective-permute-done.3 = bf16[8,32,2816]{2,1,0:T(8,128)(2,1)} collective-permute-done((bf16[8,32,2816]{2,1,0:T(8,128)(2,1)S(1)}, bf16[8,32,2816]{2,1,0:T(8,128)(2,1)}, u32[]{:S(2)}, u32[]{:S(2)}) %collective-permute-start.3) | collective-permute-done | bytes 1441824 | tf_op jit(solution)/shard_map/ppermute | solution.py:64
  72.7 264.8 %while.21 = (s32[]{:T(128)}, f32[8,64,256]{2,1,0:T(8,128)}, bf16[2,10,64,256]{3,2,1,0:T(8,128)(2,1)S(1)}, s32[8]{0:T(128)S(1)}, bf16[1,8,64,2816]{3,2,1,0:T(8,12...) while((s32[]{:T(128)}, f32[8,64,256]{2,1,0:T(8,128)}, ...), condition=%wide.region_3.4_spmd, body=%wide.region_2.3_spmd.sunk | while | flops 441188352 | bytes 35455284 | solution.py:79
  79.2 3.7 fusion.123
  89.0 6.3 %fusion.128 = bf16[44,64,4,64]{3,0,2,1:T(8,128)(2,1)S(1)} fusion(f32[64,64,44,4,1]{1,2,4,3,0:T(8,128)} %fusion.123, f32[64,64,44,4,1]{1,2,4,3,0:T(8,128)} %fusion.126, bf16[64,14,4,64,1]{3,2,0,1,4:T(4,128)(2,1)} %bitcast.261, bf16[44,4,44,4]{2,0,1,3:T(8,128)(2,1)S(1)} %get-tuple-element.315), kind=kOutput, calls=%fused_computation.38.clone.1 | convolution fusion | flops 82903040 | bytes 7733248 | tf_op jit(solution)/shard_map/while/body/eval_jaxpr/niwpj,wpvq->nviqj/dot_general | solution.py:41
  95.3 5.2 copy.133
  112.3 3.7 fusion.123
  116.8 3.7 fusion.126
  122.1 6.3 %fusion.128 = bf16[44,64,4,64]{3,0,2,1:T(8,128)(2,1)S(1)} fusion(f32[64,64,44,4,1]{1,2,4,3,0:T(8,128)} %fusion.123, f32[64,64,44,4,1]{1,2,4,3,0:T(8,128)} %fusion.126, bf16[64,14,4,64,1]{3,2,0,1,4:T(4,128)(2,1)} %bitcast.261, bf16[44,4,44,4]{2,0,1,3:T(8,128)(2,1)S(1)} %get-tuple-element.315), kind=kOutput, calls=%fused_computation.38.clone.1 | convolution fusion | flops 82903040 | bytes 7733248 | tf_op jit(solution)/shard_map/while/body/eval_jaxpr/niwpj,wpvq->nviqj/dot_general | solution.py:41
  128.4 5.2 copy.133
  145.4 3.7 fusion.123
  155.2 6.3 %fusion.128 = bf16[44,64,4,64]{3,0,2,1:T(8,128)(2,1)S(1)} fusion(f32[64,64,44,4,1]{1,2,4,3,0:T(8,128)} %fusion.123, f32[64,64,44,4,1]{1,2,4,3,0:T(8,128)} %fusion.126, bf16[64,14,4,64,1]{3,2,0,1,4:T(4,128)(2,1)} %bitcast.261, bf16[44,4,44,4]{2,0,1,3:T(8,128)(2,1)S(1)} %get-tuple-element.315), kind=kOutput, calls=%fused_computation.38.clone.1 | convolution fusion | flops 82903040 | bytes 7733248 | tf_op jit(solution)/shard_map/while/body/eval_jaxpr/niwpj,wpvq->nviqj/dot_general | solution.py:41
  161.5 5.2 copy.133
  178.5 3.7 fusion.123
  188.3 6.3 %fusion.128 = bf16[44,64,4,64]{3,0,2,1:T(8,128)(2,1)S(1)} fusion(f32[64,64,44,4,1]{1,2,4,3,0:T(8,128)} %fusion.123, f32[64,64,44,4,1]{1,2,4,3,0:T(8,128)} %fusion.126, bf16[64,14,4,64,1]{3,2,0,1,4:T(4,128)(2,1)} %bitcast.261, bf16[44,4,44,4]{2,0,1,3:T(8,128)(2,1)S(1)} %get-tuple-element.315), kind=kOutput, calls=%fused_computation.38.clone.1 | convolution fusion | flops 82903040 | bytes 7733248 | tf_op jit(solution)/shard_map/while/body/eval_jaxpr/niwpj,wpvq->nviqj/dot_general | solution.py:41
  194.6 5.2 copy.133
  211.6 3.7 fusion.123
  216.1 3.7 fusion.126
  221.4 6.3 %fusion.128 = bf16[44,64,4,64]{3,0,2,1:T(8,128)(2,1)S(1)} fusion(f32[64,64,44,4,1]{1,2,4,3,0:T(8,128)} %fusion.123, f32[64,64,44,4,1]{1,2,4,3,0:T(8,128)} %fusion.126, bf16[64,14,4,64,1]{3,2,0,1,4:T(4,128)(2,1)} %bitcast.261, bf16[44,4,44,4]{2,0,1,3:T(8,128)(2,1)S(1)} %get-tuple-element.315), kind=kOutput, calls=%fused_computation.38.clone.1 | convolution fusion | flops 82903040 | bytes 7733248 | tf_op jit(solution)/shard_map/while/body/eval_jaxpr/niwpj,wpvq->nviqj/dot_general | solution.py:41
  227.7 5.2 copy.133
  244.7 3.7 fusion.123
  249.2 3.7 fusion.126
  254.5 6.3 %fusion.128 = bf16[44,64,4,64]{3,0,2,1:T(8,128)(2,1)S(1)} fusion(f32[64,64,44,4,1]{1,2,4,3,0:T(8,128)} %fusion.123, f32[64,64,44,4,1]{1,2,4,3,0:T(8,128)} %fusion.126, bf16[64,14,4,64,1]{3,2,0,1,4:T(4,128)(2,1)} %bitcast.261, bf16[44,4,44,4]{2,0,1,3:T(8,128)(2,1)S(1)} %get-tuple-element.315), kind=kOutput, calls=%fused_computation.38.clone.1 | convolution fusion | flops 82903040 | bytes 7733248 | tf_op jit(solution)/shard_map/while/body/eval_jaxpr/niwpj,wpvq->nviqj/dot_general | solution.py:41
  260.8 5.2 copy.133
  277.9 3.7 fusion.123
  287.6 6.3 %fusion.128 = bf16[44,64,4,64]{3,0,2,1:T(8,128)(2,1)S(1)} fusion(f32[64,64,44,4,1]{1,2,4,3,0:T(8,128)} %fusion.123, f32[64,64,44,4,1]{1,2,4,3,0:T(8,128)} %fusion.126, bf16[64,14,4,64,1]{3,2,0,1,4:T(4,128)(2,1)} %bitcast.261, bf16[44,4,44,4]{2,0,1,3:T(8,128)(2,1)S(1)} %get-tuple-element.315), kind=kOutput, calls=%fused_computation.38.clone.1 | convolution fusion | flops 82903040 | bytes 7733248 | tf_op jit(solution)/shard_map/while/body/eval_jaxpr/niwpj,wpvq->nviqj/dot_general | solution.py:41
  293.9 5.2 copy.133
  310.9 3.7 fusion.123
  315.4 3.7 fusion.126
  320.7 6.3 %fusion.128 = bf16[44,64,4,64]{3,0,2,1:T(8,128)(2,1)S(1)} fusion(f32[64,64,44,4,1]{1,2,4,3,0:T(8,128)} %fusion.123, f32[64,64,44,4,1]{1,2,4,3,0:T(8,128)} %fusion.126, bf16[64,14,4,64,1]{3,2,0,1,4:T(4,128)(2,1)} %bitcast.261, bf16[44,4,44,4]{2,0,1,3:T(8,128)(2,1)S(1)} %get-tuple-element.315), kind=kOutput, calls=%fused_computation.38.clone.1 | convolution fusion | flops 82903040 | bytes 7733248 | tf_op jit(solution)/shard_map/while/body/eval_jaxpr/niwpj,wpvq->nviqj/dot_general | solution.py:41
  327.0 5.2 copy.133
  338.4 271.0 %while.20 = (s32[]{:T(128)}, f32[8,64,256]{2,1,0:T(8,128)}, bf16[2,10,64,256]{3,2,1,0:T(8,128)(2,1)S(1)}, s32[8]{0:T(128)S(1)}, bf16[8,64,2816]{2,1,0:T(8,128)(2...) while((s32[]{:T(128)}, f32[8,64,256]{2,1,0:T(8,128)}, ...), condition=%wide.region_1.2_spmd, body=%wide.region_0.1_spmd.sunk | while | flops 441188352 | bytes 42242408 | solution.py:88
  344.8 4.6 fusion.105
  350.1 4.5 fusion.108
  356.3 6.3 %fusion.110 = bf16[44,64,4,64]{3,0,2,1:T(8,128)(2,1)S(1)} fusion(f32[64,64,44,4,1]{1,2,4,3,0:T(8,128)} %fusion.105, f32[64,64,44,4,1]{1,2,4,3,0:T(8,128)} %fusion.108, bf16[64,14,4,64,1]{3,2,0,1,4:T(4,128)(2,1)} %bitcast.262, bf16[44,4,44,4]{2,0,1,3:T(8,128)(2,1)} %copy-done), kind=kOutput, calls=%fused_computation.3.clone.1 | convolution fusion | flops 82903040 | bytes 15007744 | tf_op jit(solution)/shard_map/while/body/eval_jaxpr/niwpj,wpvq->nviqj/dot_general | solution.py:41
  362.6 5.2 copy.125
  378.7 4.6 fusion.105
  384.0 4.5 fusion.108
  390.1 6.3 %fusion.110 = bf16[44,64,4,64]{3,0,2,1:T(8,128)(2,1)S(1)} fusion(f32[64,64,44,4,1]{1,2,4,3,0:T(8,128)} %fusion.105, f32[64,64,44,4,1]{1,2,4,3,0:T(8,128)} %fusion.108, bf16[64,14,4,64,1]{3,2,0,1,4:T(4,128)(2,1)} %bitcast.262, bf16[44,4,44,4]{2,0,1,3:T(8,128)(2,1)} %copy-done), kind=kOutput, calls=%fused_computation.3.clone.1 | convolution fusion | flops 82903040 | bytes 15007744 | tf_op jit(solution)/shard_map/while/body/eval_jaxpr/niwpj,wpvq->nviqj/dot_general | solution.py:41
  396.5 5.2 copy.125
  412.5 4.6 fusion.105
  417.9 4.5 fusion.108
  424.0 6.3 %fusion.110 = bf16[44,64,4,64]{3,0,2,1:T(8,128)(2,1)S(1)} fusion(f32[64,64,44,4,1]{1,2,4,3,0:T(8,128)} %fusion.105, f32[64,64,44,4,1]{1,2,4,3,0:T(8,128)} %fusion.108, bf16[64,14,4,64,1]{3,2,0,1,4:T(4,128)(2,1)} %bitcast.262, bf16[44,4,44,4]{2,0,1,3:T(8,128)(2,1)} %copy-done), kind=kOutput, calls=%fused_computation.3.clone.1 | convolution fusion | flops 82903040 | bytes 15007744 | tf_op jit(solution)/shard_map/while/body/eval_jaxpr/niwpj,wpvq->nviqj/dot_general | solution.py:41
  430.4 5.2 copy.125
  446.4 4.6 fusion.105
  451.8 4.5 fusion.108
  457.9 6.3 %fusion.110 = bf16[44,64,4,64]{3,0,2,1:T(8,128)(2,1)S(1)} fusion(f32[64,64,44,4,1]{1,2,4,3,0:T(8,128)} %fusion.105, f32[64,64,44,4,1]{1,2,4,3,0:T(8,128)} %fusion.108, bf16[64,14,4,64,1]{3,2,0,1,4:T(4,128)(2,1)} %bitcast.262, bf16[44,4,44,4]{2,0,1,3:T(8,128)(2,1)} %copy-done), kind=kOutput, calls=%fused_computation.3.clone.1 | convolution fusion | flops 82903040 | bytes 15007744 | tf_op jit(solution)/shard_map/while/body/eval_jaxpr/niwpj,wpvq->nviqj/dot_general | solution.py:41
  464.2 5.2 copy.125
  480.3 4.6 fusion.105
  485.7 4.5 fusion.108
  491.8 6.3 %fusion.110 = bf16[44,64,4,64]{3,0,2,1:T(8,128)(2,1)S(1)} fusion(f32[64,64,44,4,1]{1,2,4,3,0:T(8,128)} %fusion.105, f32[64,64,44,4,1]{1,2,4,3,0:T(8,128)} %fusion.108, bf16[64,14,4,64,1]{3,2,0,1,4:T(4,128)(2,1)} %bitcast.262, bf16[44,4,44,4]{2,0,1,3:T(8,128)(2,1)} %copy-done), kind=kOutput, calls=%fused_computation.3.clone.1 | convolution fusion | flops 82903040 | bytes 15007744 | tf_op jit(solution)/shard_map/while/body/eval_jaxpr/niwpj,wpvq->nviqj/dot_general | solution.py:41
  498.1 5.2 copy.125
  514.2 4.6 fusion.105
  519.5 4.5 fusion.108
  525.6 6.3 %fusion.110 = bf16[44,64,4,64]{3,0,2,1:T(8,128)(2,1)S(1)} fusion(f32[64,64,44,4,1]{1,2,4,3,0:T(8,128)} %fusion.105, f32[64,64,44,4,1]{1,2,4,3,0:T(8,128)} %fusion.108, bf16[64,14,4,64,1]{3,2,0,1,4:T(4,128)(2,1)} %bitcast.262, bf16[44,4,44,4]{2,0,1,3:T(8,128)(2,1)} %copy-done), kind=kOutput, calls=%fused_computation.3.clone.1 | convolution fusion | flops 82903040 | bytes 15007744 | tf_op jit(solution)/shard_map/while/body/eval_jaxpr/niwpj,wpvq->nviqj/dot_general | solution.py:41
  532.0 5.2 copy.125
  548.0 4.6 fusion.105
  553.4 4.5 fusion.108
  559.5 6.3 %fusion.110 = bf16[44,64,4,64]{3,0,2,1:T(8,128)(2,1)S(1)} fusion(f32[64,64,44,4,1]{1,2,4,3,0:T(8,128)} %fusion.105, f32[64,64,44,4,1]{1,2,4,3,0:T(8,128)} %fusion.108, bf16[64,14,4,64,1]{3,2,0,1,4:T(4,128)(2,1)} %bitcast.262, bf16[44,4,44,4]{2,0,1,3:T(8,128)(2,1)} %copy-done), kind=kOutput, calls=%fused_computation.3.clone.1 | convolution fusion | flops 82903040 | bytes 15007744 | tf_op jit(solution)/shard_map/while/body/eval_jaxpr/niwpj,wpvq->nviqj/dot_general | solution.py:41
  565.9 5.2 copy.125
  581.9 4.6 fusion.105
  587.3 4.5 fusion.108
  593.4 6.3 %fusion.110 = bf16[44,64,4,64]{3,0,2,1:T(8,128)(2,1)S(1)} fusion(f32[64,64,44,4,1]{1,2,4,3,0:T(8,128)} %fusion.105, f32[64,64,44,4,1]{1,2,4,3,0:T(8,128)} %fusion.108, bf16[64,14,4,64,1]{3,2,0,1,4:T(4,128)(2,1)} %bitcast.262, bf16[44,4,44,4]{2,0,1,3:T(8,128)(2,1)} %copy-done), kind=kOutput, calls=%fused_computation.3.clone.1 | convolution fusion | flops 82903040 | bytes 15007744 | tf_op jit(solution)/shard_map/while/body/eval_jaxpr/niwpj,wpvq->nviqj/dot_general | solution.py:41
  599.7 5.2 copy.125
  (415 shorter events, 199.8 us)
Async XLA Ops:
  6.5 30.3 %copy-start.6 = (bf16[8,64,256]{2,1,0:T(8,128)(2,1)S(1)}, bf16[8,64,256]{2,1,0:T(8,128)(2,1)}, u32[]{:S(2)}) copy-start(bf16[8,64,256]{2,1,0:T(8,128)(2,1)} %param.16) | copy-start | bytes 786436
  6.5 30.3 %copy-start.7 = (bf16[1,8,64,256]{3,2,1,0:T(8,128)(2,1)S(1)}, bf16[1,8,64,256]{3,2,1,0:T(8,128)(2,1)}, u32[]{:S(2)}) copy-start(bf16[1,8,64,256]{3,2,1,0:T(8,128)(2,1)} %param.15) | copy-start | bytes 786436
  6.5 28.1 %copy-start.11 = (s32[8]{0:T(128)S(1)}, s32[8]{0:T(128)}, u32[]{:S(2)}) copy-start(s32[8]{0:T(128)} %param.19) | copy-start | bytes 100
  6.5 30.2 %copy-start.8 = (bf16[44,4,44,4]{2,3,1,0:T(4,128)(2,1)S(1)}, bf16[44,4,44,4]{2,3,1,0:T(4,128)(2,1)}, u32[]{:S(2)}) copy-start(bf16[44,4,44,4]{2,3,1,0:T(4,128)(2,1)} %param.17) | copy-start | bytes 185860
  6.5 331.0 %all-gather.2.cloned.1.call-start = ((), (), s32[]{:S(2)}) async-start(), calls=%async_computation | async-start | bytes 3604480 | tf_op jit(solution)/shard_map/all_gather | solution.py:80
  6.6 19.4 %collective-permute-start.2 = (bf16[8,16,2816]{2,1,0:T(8,128)(2,1)}, bf16[8,16,2816]{2,1,0:T(8,128)(2,1)S(1)}, u32[]{:S(2)}, u32[]{:S(2)}) collective-permute-start(bf16[8,16,2816]{2,1,0:T(8,128)(2,1)} %param.13), channel_id=1, source_target_pairs={{0,8},{8,0},{16,24},{24,16},{1,9},{9,1},{17,25},{25,17},{2,10},{10... | collective-permute-start | bytes 2162696 | tf_op jit(solution)/shard_map/ppermute | solution.py:64
  27.6 40.7 %collective-permute-start.3 = (bf16[8,32,2816]{2,1,0:T(8,128)(2,1)S(1)}, bf16[8,32,2816]{2,1,0:T(8,128)(2,1)}, u32[]{:S(2)}, u32[]{:S(2)}) collective-permute-start(bf16[8,32,2816]{2,1,0:T(8,128)(2,1)S(1)} %maximum_select_fusion.1), channel_id=1, source_target_pairs={{0,16},{8,24},{16,0},{24,8},{1,17},{9,25},{17,1},{25,9},{2,18},{10... | collective-permute-start | bytes 4325384 | tf_op jit(solution)/shard_map/ppermute | solution.py:64
  30.3 6.5 %collective-permute-start.1 = (bf16[2,1,64,256]{3,2,1,0:T(8,128)(2,1)S(1)}, bf16[2,1,64,256]{3,2,1,0:T(8,128)(2,1)S(1)}, u32[]{:S(2)}, u32[]{:S(2)}) collective-permute-start(bf16[2,1,64,256]{3,2,1,0:T(8,128)(2,1)S(1)} %get-tuple-element.146), channel_id=1, source_target_pairs={{1,0},{2,1},{3,2},{4,3},{5,4},{6,5},{7,6},{9,8},{10,9},{11,10},{12... | collective-permute-start | bytes 196616 | tf_op jit(solution)/shard_map/ppermute | solution.py:16
  31.6 5.2 collective-permute-start
  72.7 5.8 copy-start.2
  101.5 4.3 copy-start.3
  105.8 5.8 copy-start.2
  134.6 4.3 copy-start.3
  138.9 5.8 copy-start.2
  167.7 4.3 copy-start.3
  172.0 5.8 copy-start.2
  200.8 4.3 copy-start.3
  205.1 5.8 copy-start.2
  233.9 4.3 copy-start.3
  238.2 5.8 copy-start.2
  267.0 4.3 copy-start.3
  271.3 5.8 copy-start.2
  300.1 4.3 copy-start.3
  304.4 5.8 copy-start.2
  333.2 4.3 copy-start.3
  338.4 271.0 %copy-start.9 = (pred[8,256]{1,0:T(8,128)(4,1)S(1)}, pred[8,256]{1,0:T(8,128)(4,1)}, u32[]{:S(2)}) copy-start(pred[8,256]{1,0:T(8,128)(4,1)} %broadcast_compare_fusion) | copy-start | bytes 6148
  338.4 271.0 %copy-start.10 = (pred[8,64]{1,0:T(8,128)(4,1)S(1)}, pred[8,64]{1,0:T(8,128)(4,1)}, u32[]{:S(2)}) copy-start(pred[8,64]{1,0:T(8,128)(4,1)} %iota_compare_fusion) | copy-start | bytes 1540
  338.4 2.6 copy-start
  338.4 5.7 copy-start.4
  367.8 4.4 copy-start.5
  368.4 3.8 copy-start.1
  372.2 2.7 copy-start
  372.2 5.8 copy-start.4
  401.7 4.4 copy-start.5
  402.3 3.8 copy-start.1
  406.1 2.7 copy-start
  406.1 5.8 copy-start.4
  435.6 4.4 copy-start.5
  436.1 3.8 copy-start.1
  440.0 2.7 copy-start
  440.0 5.8 copy-start.4
  469.5 4.4 copy-start.5
  470.0 3.8 copy-start.1
  473.8 2.7 copy-start
  473.8 5.8 copy-start.4
  503.3 4.4 copy-start.5
  503.9 3.8 copy-start.1
  507.7 2.7 copy-start
  507.7 5.8 copy-start.4
  537.2 4.4 copy-start.5
  537.8 3.8 copy-start.1
  541.6 2.7 copy-start
  541.6 5.8 copy-start.4
  571.1 4.4 copy-start.5
  571.7 3.8 copy-start.1
  575.5 2.7 copy-start
  575.5 5.8 copy-start.4
  605.0 4.4 copy-start.5
  605.5 3.8 copy-start.1
Sparse Core Ops, SparseCore 0:
  34.7 49.9 all-gather.1
